TPU v7x, 512 devices: a whole 4x4x16 slice. The times are simulated.
512 devices in a mesh: pool: 64 (over z, y), head: 8 (over x, core).
Axes of the slice: x: 4, y: 4, z: 16, core: 2. Of those that a mesh axis runs over, the one named last changes fastest.
Arguments:
- kv_store: bfloat16 [128, 2, 64, 1024], P('pool', None, None, 'head'), may hold values from -6 to 6
- fresh_q: bfloat16 [64, 24, 8192], P('pool', None, 'head'), may hold values from -160 to 160
- fresh_kv: bfloat16 [64, 24, 2, 1024], P('pool', None, None, 'head'), may hold values from -6 to 6
- dec_q: bfloat16 [32, 8192], P(None, 'head'), may hold values from -160 to 160
- dec_kv: bfloat16 [32, 2, 1024], P(None, None, 'head'), may hold values from -6 to 6
- out_weight: bfloat16 [8192, 8192], P('head', 'pool'), may hold values from -0.0625 to 0.0625
- span_slot: int32 [64], replicated, may hold values from 0 to 127, as said below
- span_order: int32 [64], replicated, may hold values from 0 to 63, each once
- span_start: int32 [64], replicated, may hold values from 0 to 4536, as said below
- pick: int32 [64, 24], replicated, may hold values from 0 to 63, as said below
- dec_len: int32 [32], replicated, may hold values from 1 to 64, as said below
Outputs:
- fresh_out: bfloat16 [64, 24, 8192], P('pool', None, 'head')
- dec_proj: bfloat16 [32, 8192], P(None, 'pool')
Inputs may be any that keep to these rules, and one draw needn't show every extreme that they name: `span_slot`: distinct values. Storage rows k * 2 to (k + 1) * 2 - 1 belong to pool device k; some device holds 2 spans in every draw. span_start[0] = 0 and span_start[s + 1] - span_start[s] lies between 64 and 80. `pick`: each row holds 24 distinct indices in increasing order. `dec_len`: some row reads all 64 slots in every draw.
All inputs are finite; a program needn't handle non-finite values.
Results may differ from a plain program's by a relative error of at most 0.018.
Values may be sent and summed in bfloat16 or wider, within the bound.
A program may use at most 64 MiB of HBM per device.

v0:
```python
import jax
import jax.numpy as jnp
from jax import lax
from jax.sharding import PartitionSpec as P

QH = 64
KVH = 8
HD = 128
L = 64
R = 24
NEG = -1e30
BASE = 500000.0


def merged_2(value, axis, combine):
    everything = jax.tree.map(
        lambda part, kind: lax.all_gather(part.astype(kind), axis),
        value,
        jax.tree.map(lambda a: jnp.bfloat16 if a.dtype == jnp.float32 else a.dtype, value),
    )

    def take(k):
        return jax.tree.map(lambda part, own: part[k].astype(own.dtype), everything, value)

    return lax.fori_loop(
        1, lax.axis_size(axis), lambda k, so_far: combine(so_far, take(k)), take(0)
    )


def frequencies(half):
    return jnp.power(BASE, -jnp.arange(half, dtype=jnp.float32) / half)


def rotate(heads, positions):
    half = heads.shape[-1] // 2
    angle = positions.astype(jnp.float32)[:, None, None] * frequencies(half)
    cosine = jnp.cos(angle)
    sine = jnp.sin(angle)
    first = heads[..., :half]
    second = heads[..., half:]
    return jnp.concatenate(
        [first * cosine - second * sine, second * cosine + first * sine], axis=-1
    )


def to_groups(rows_in, group):
    count = rows_in.shape[0]
    shaped = rows_in.reshape(count, -1, group, HD)
    local = shaped.shape[1]
    return shaped.transpose(1, 0, 2, 3).reshape(local, count * group, HD)


def from_groups(merged, count, group):
    local = merged.shape[0]
    return (
        merged.reshape(local, count, group, HD)
        .transpose(1, 0, 2, 3)
        .reshape(count, local * group * HD)
    )


def by_head(rows_in):
    count = rows_in.shape[0]
    return rows_in.reshape(count, -1, HD).transpose(1, 0, 2)


def empty_state(local, count):
    return (
        jnp.full((local, count), NEG, jnp.float32),
        jnp.zeros((local, count), jnp.float32),
        jnp.zeros((local, count, HD), jnp.float32),
    )


def absorb(state, queries, key_block, value_block, visible):
    highest, total, accum = state
    scale = HD ** (-0.5)
    scores = (
        jnp.einsum("gqd,gkd->gqk", queries, key_block, preferred_element_type=jnp.float32) * scale
    )
    scores = jnp.where(visible[None], scores, NEG)
    raised = jnp.maximum(highest, jnp.max(scores, axis=-1))
    weights = jnp.where(visible[None], jnp.exp(scores - raised[..., None]), 0.0)
    factor = jnp.exp(highest - raised)
    total = total * factor + jnp.sum(weights, axis=-1)
    accum = accum * factor[..., None] + jnp.einsum(
        "gqk,gkd->gqd",
        weights.astype(jnp.bfloat16),
        value_block,
        preferred_element_type=jnp.float32,
    )
    return (raised, total, accum)


def combine(first, second):
    raised = jnp.maximum(first[0], second[0])
    left = jnp.exp(first[0] - raised)
    right = jnp.exp(second[0] - raised)
    return (
        raised,
        first[1] * left + second[1] * right,
        first[2] * left[..., None] + second[2] * right[..., None],
    )


def shards(
    kv_store,
    fresh_q,
    fresh_kv,
    dec_q,
    dec_kv,
    out_weight,
    span_slot,
    span_order,
    span_start,
    pick,
    dec_len,
):
    group = QH // KVH
    my_slot = lax.axis_index("pool")
    slots = span_order.shape[0]
    stored = kv_store.shape[0]
    store_total = stored * lax.axis_size("pool")
    local = fresh_kv.shape[-1] // HD
    rows = dec_q.shape[0]
    span_ids = jnp.arange(slots, dtype=jnp.int32)
    span_place = jnp.sum(
        jnp.where(span_order[None, :] == span_ids[:, None], span_ids[None, :], 0), axis=1
    )
    store_ids = jnp.arange(store_total, dtype=jnp.int32)
    holding = span_slot[None, :] == store_ids[:, None]
    store_live = jnp.any(holding, axis=1)
    store_place = jnp.sum(jnp.where(holding, span_place[None, :], 0), axis=1)
    columns = jnp.arange(L, dtype=jnp.int32)
    picked = jnp.any(pick[:, :, None] == columns[None, None, :], axis=1)
    own_pick = lax.dynamic_index_in_dim(pick, my_slot, 0, keepdims=False)
    own_start = lax.dynamic_index_in_dim(span_start, my_slot, 0, keepdims=False)
    query_place = own_start + own_pick
    rotated_q = rotate(fresh_q[0].reshape(R, -1, HD).astype(jnp.float32), query_place).astype(
        jnp.bfloat16
    )
    queries = to_groups(rotated_q.reshape(R, -1), group)
    query_reach = jnp.repeat(query_place, group)
    every_fresh = lax.all_gather(fresh_kv, "pool", axis=0, tiled=True)
    fresh_place = (span_start[:, None] + pick).reshape(-1)
    turned_fresh = rotate(
        every_fresh[:, :, 0].reshape(slots * R, -1, HD).astype(jnp.float32), fresh_place
    ).astype(jnp.bfloat16)
    fresh_keys = by_head(turned_fresh.reshape(slots * R, -1))
    fresh_values = by_head(every_fresh[:, :, 1].reshape(slots * R, -1))
    recompute_state = absorb(
        empty_state(local, R * group),
        queries,
        fresh_keys,
        fresh_values,
        fresh_place[None, :] <= query_reach[:, None],
    )
    dec_queries = to_groups(dec_q, group)
    row_len = jnp.repeat(dec_len, group)

    def view(item, place):
        turned = rotate(
            item[0].reshape(L, -1, HD).astype(jnp.float32), jnp.full((L,), span_start[place])
        ).astype(jnp.bfloat16)
        reach = span_start[place] + columns
        keep = jnp.logical_not(lax.dynamic_index_in_dim(picked, place, 0, keepdims=False))
        return (by_head(turned.reshape(L, -1)), by_head(item[1]), reach, keep)

    initial = (recompute_state,)

    def wanted(place):
        return place <= my_slot

    def block_step(carry, key_block, value_block, reach, keep):
        seen = keep[None, :] & (reach[None, :] <= query_reach[:, None])
        return (absorb(carry[0], queries, key_block, value_block, seen),)

    piece = lax.all_gather(kv_store, "pool", axis=0, tiled=True)

    def one_row(inner, inputs):
        item, index = inputs
        place = store_place[index]

        def apply(state_in):
            key_block, value_block, reach, keep = view(item, place)
            return block_step(state_in, key_block, value_block, reach, keep)

        return (
            lax.cond(store_live[index] & wanted(place), apply, lambda state_in: state_in, inner),
            None,
        )

    indices = jnp.arange(piece.shape[0], dtype=jnp.int32)
    result, _ = lax.scan(one_row, initial, (piece, indices))
    own_keys = lax.dynamic_slice_in_dim(fresh_keys, my_slot * R, R, 1)
    own_values = lax.dynamic_slice_in_dim(fresh_values, my_slot * R, R, 1)
    seen_fresh = jnp.broadcast_to((my_slot < row_len)[:, None], (rows * group, R))
    dec_state = absorb(
        empty_state(local, rows * group), dec_queries, own_keys, own_values, seen_fresh
    )

    def make_apply(item, place):

        def apply(state_in):
            key_block, value_block, reach, keep = view(item, place)
            return absorb(
                state_in,
                dec_queries,
                key_block,
                value_block,
                keep[None, :] & (place < row_len)[:, None],
            )

        return apply

    for offset in range(stored):
        index = my_slot * stored + offset
        place = store_place[index]
        dec_state = lax.cond(
            store_live[index],
            make_apply(kv_store[offset], place),
            lambda state_in: state_in,
            dec_state,
        )
    dec_state = merged_2(dec_state, "pool", combine)
    recompute_final = result[0]
    attended = recompute_final[2] / recompute_final[1][..., None]
    fresh_out = from_groups(attended, R, group).astype(jnp.bfloat16)[None]
    token_keys = by_head(dec_kv[:, 0])
    token_values = by_head(dec_kv[:, 1])
    token_seen = (jnp.arange(rows * group, dtype=jnp.int32) // group)[:, None] == jnp.arange(
        rows, dtype=jnp.int32
    )[None, :]
    dec_state = absorb(dec_state, dec_queries, token_keys, token_values, token_seen)
    dec_attn = from_groups(dec_state[2] / dec_state[1][..., None], rows, group).astype(jnp.bfloat16)
    partial_terms = jnp.dot(dec_attn, out_weight, preferred_element_type=jnp.float32)
    dec_proj = lax.psum(partial_terms, "head").astype(jnp.bfloat16)
    return (fresh_out, dec_proj)


def solution(mesh):
    return jax.shard_map(
        shards,
        mesh=mesh,
        in_specs=(
            P("pool", None, None, "head"),
            P("pool", None, "head"),
            P("pool", None, None, "head"),
            P(None, "head"),
            P(None, None, "head"),
            P("head", "pool"),
            P(),
            P(),
            P(),
            P(),
            P(),
        ),
        out_specs=(P("pool", None, "head"), P(None, "pool")),
        check_vma=False,
    )
```

profile of v0, /device:TPU:504, one launch (start us, length us, event | category | flops | bytes accessed | tf_op | source)
XLA Modules:
  0.0 1444.8 jit_solution(17761273239110863424)
XLA Ops:
  17.9 92.9 %all_gather.24 = bf16[64,24,2,128]{3,1,0,2:T(8,128)(2,1)S(1)} all-gather(bf16[1,24,2,128]{3,1,0,2:T(8,128)(2,1)S(1)} %copy.26), channel_id=1, replica_groups=mesh['pool'=64,'head'=8] {'pool'}, dimensions={0}, use_global_device_ids=true | all-gather | bytes 798720 | tf_op jit(solution)/shard_map/all_gather | solution.py:144
  123.2 84.3 %all-gather.3 = bf16[64,1,256]{2,1,0:T(2,128)(2,1)S(1)} all-gather(bf16[1,1,256]{2,1,0:T(2,128)(2,1)S(1)} %convert_bitcast_fusion.2), channel_id=2, replica_groups=mesh['pool'=64,'head'=8] {'pool'}, dimensions={0}, use_global_device_ids=true | all-gather | bytes 33280 | tf_op jit(solution)/shard_map/all_gather | solution.py:17
  207.5 79.9 %all-gather.4 = bf16[64,1,256]{2,1,0:T(2,128)(2,1)S(1)} all-gather(bf16[1,1,256]{2,1,0:T(2,128)(2,1)S(1)} %convert_bitcast_fusion.1), channel_id=3, replica_groups=mesh['pool'=64,'head'=8] {'pool'}, dimensions={0}, use_global_device_ids=true | all-gather | bytes 33280 | tf_op jit(solution)/shard_map/all_gather | solution.py:17
  289.7 1055.2 %while.35 = (s32[]{:T(128)}, f32[1,192]{1,0:T(1,128)S(1)}, f32[1,192]{1,0:T(1,128)S(1)}, f32[1,192,128]{2,1,0:T(8,128)S(1)}, s32[128]{0:T(128)S(1)}, /*index=5*/...) while((s32[]{:T(128)}, f32[1,192]{1,0:T(1,128)S(1)}, ...), condition=%wide.region_11.12_spmd.clone, body=%wide.region_6.11_spmd.clone.sunk | while | flops 6599373 | bytes 545140 | solution.py:194
  326.5 6.3 conditional.7
  337.9 6.3 conditional.7
  349.3 6.3 conditional.7
  360.7 6.3 conditional.7
  377.2 6.3 conditional.7
  388.6 6.3 conditional.7
  458.4 6.3 conditional.7
  469.8 6.3 conditional.7
  481.2 6.3 conditional.7
  507.8 6.3 conditional.7
  519.2 6.3 conditional.7
  530.6 6.3 conditional.7
  547.1 6.3 conditional.7
  558.5 6.3 conditional.7
  570.0 6.3 conditional.7
  591.5 6.3 conditional.7
  667.6 6.3 conditional.7
  679.0 6.3 conditional.7
  690.4 6.3 conditional.7
  854.1 6.3 conditional.7
  963.1 6.3 conditional.7
  1053.2 6.3 conditional.7
  1087.4 6.3 conditional.7
  1181.2 6.3 conditional.7
  1310.6 6.3 conditional.7
  1338.5 6.3 conditional.7
  1346.5 66.8 %while.34 = (s32[]{:T(128)}, f32[1,256]{1,0:T(1,128)S(1)}, f32[1,256]{1,0:T(1,128)S(1)}, f32[1,256,128]{2,1,0:T(8,128)S(1)}, bf16[64,1,256]{2,1,0:T(2,128)(2,1)S...) while((s32[]{:T(128)}, f32[1,256]{1,0:T(1,128)S(1)}, ...), condition=%wide.region_23.24_spmd, body=%wide.region_22.23_spmd.sunk | while | flops 133125 | bytes 337047 | solution.py:25
  1413.8 24.1 %psum.7 = bf16[32,128]{1,0:T(8,128)(2,1)} all-reduce(f32[32,128]{1,0:T(8,128)S(1)} %fusion.141), channel_id=1, replica_groups=mesh['pool'=64,'head'=8] {'head'}, use_global_device_ids=true, to_apply=%region_26.27 | all-reduce | flops 4096 | bytes 24576 | tf_op jit(solution)/shard_map/psum | solution.py:237
  (1729 shorter events, 816.6 us)
Async XLA Ops:
  7.2 1406.5 %copy-start = (bf16[1024,128]{1,0:T(8,128)(2,1)S(1)}, bf16[1024,128]{1,0:T(8,128)(2,1)}, u32[]{:S(2)}) copy-start(bf16[1024,128]{1,0:T(8,128)(2,1)} %param.26) | copy-start | bytes 786436
  7.2 282.5 %all-gather.8.cloned.1.call-start = ((), (), s32[]{:S(2)}) async-start(), calls=%async_computation | async-start | bytes 4259840 | tf_op jit(solution)/shard_map/all_gather | solution.py:178
  7.9 1337.7 %all-gather.10.cloned.1.call-start = ((), (), s32[]{:S(2)}) async-start(), calls=%async_computation.1 | async-start | bytes 4259840 | tf_op jit(solution)/shard_map/all_gather | solution.py:17
  110.9 4.5 copy-start.1
  114.6 0.9 copy-start.5
  114.8 6.6 copy-start.4
  115.1 7.0 copy-start.2
  288.7 0.7 copy-start.3
Sparse Core Ops, SparseCore 0:
  10.9 141.0 all-gather.7
  154.9 140.6 all-gather.9
where the time goes:
time: 1470 us; the launch traced here: 1440 us
  loops' own time  579 us (39%)
  local copies, waits for them, and re-layouts  303 us (21%)
  blocking collectives  281 us (19%)
  other arithmetic  184 us (13%)
  matrix products  81.1 us (6%)
  between operations  15.7 us (1%)
    another operation x1, loops' own time, shards(): result, _ = lax.scan(one_row, initial, (piece, indices))  406 us
    another operation x128, loops' own time, one_row(): lax.cond(store_live[index] & wanted(place), apply, lambda state_in: state...  169 us
    all_gather x2, blocking collectives, merged_2(): lax.all_gather(part.astype(kind), axis)  164 us
    all_gather x1, blocking collectives, shards(): every_fresh = lax.all_gather(fresh_kv, 'pool', axis=0, tiled=True)  92.9 us
    dynamic_slice x128, local copies, waits for them, and re-layouts, shards(): result, _ = lax.scan(one_row, initial, (piece, indices))  82.3 us
    dynamic_slice x128, local copies, waits for them, and re-layouts, one_row(): place = store_place[index]  81.7 us
    dynamic_slice x128, local copies, waits for them, and re-layouts, one_row(): store_live[index] & wanted(place)  78.2 us
    dot_general x68, matrix products, absorb(): jnp.einsum('gqk,gkd->gqd', weights.astype(jnp.bfloat16), value_block, pre...  66.1 us
  transfers between devices with their start and end apart: 2, of which 0 were waited for; matrix products, arithmetic and copies ran while one was open for 35% of the time, Pallas kernels for 0%

commit v1 on v0

--- a/solution.py
+++ b/solution.py
@@ -141,7 +141,8 @@
     )
     queries = to_groups(rotated_q.reshape(R, -1), group)
     query_reach = jnp.repeat(query_place, group)
-    every_fresh = lax.all_gather(fresh_kv, "pool", axis=0, tiled=True)
+    sent = jnp.stack([fresh_kv] * lax.axis_size("pool"))
+    every_fresh = jnp.concatenate(lax.all_to_all(sent, "pool", 0, 0), axis=0)
     fresh_place = (span_start[:, None] + pick).reshape(-1)
     turned_fresh = rotate(
         every_fresh[:, :, 0].reshape(slots * R, -1, HD).astype(jnp.float32), fresh_place

time: 1470 us -> 1420 us (0.966)
  blocking collectives: 281 us -> 190 us
  waiting for transfers between devices: 0.72 us -> 40 us
    all_gather x1 -> x0, blocking collectives: 92.9 us -> none  [shards(): every_fresh = lax.all_gather(fresh_kv, 'pool', axis=0, tiled=True)]
    all_to_all x0 -> x1, waiting for transfers between devices: none -> 39.3 us  [shards(): every_fresh = jnp.concatenate(lax.all_to_all(sent, 'pool', 0, 0), axis=0)]
  transfers between devices with their start and end apart: 2 -> 3, of which waited for: 0 -> 1; matrix products, arithmetic and copies ran while one was open for 35% -> 36% of each run, Pallas kernels for 0% -> 0%
where the time goes in v1:
time: 1420 us; the launch traced here: 1400 us
  loops' own time  579 us (41%)
  local copies, waits for them, and re-layouts  301 us (21%)
  blocking collectives  190 us (13%)
  other arithmetic  182 us (13%)
  matrix products  81.1 us (6%)
  waiting for transfers between devices  40 us (3%)
  between operations  15.6 us (1%)
    another operation x1, loops' own time, shards(): result, _ = lax.scan(one_row, initial, (piece, indices))  406 us
    another operation x128, loops' own time, one_row(): lax.cond(store_live[index] & wanted(place), apply, lambda state_in: state...  169 us
    all_gather x2, blocking collectives, merged_2(): lax.all_gather(part.astype(kind), axis)  166 us
    dynamic_slice x128, local copies, waits for them, and re-layouts, shards(): result, _ = lax.scan(one_row, initial, (piece, indices))  82.3 us
    dynamic_slice x128, local copies, waits for them, and re-layouts, one_row(): place = store_place[index]  81.7 us
    dynamic_slice x128, local copies, waits for them, and re-layouts, one_row(): store_live[index] & wanted(place)  78.2 us
    dot_general x68, matrix products, absorb(): jnp.einsum('gqk,gkd->gqd', weights.astype(jnp.bfloat16), value_block, pre...  66.1 us
    add x63, other arithmetic, combine(): first[2] * left[..., None] + second[2] * right[..., None]  63.3 us
  transfers between devices with their start and end apart: 3, of which 1 were waited for; matrix products, arithmetic and copies ran while one was open for 36% of the time, Pallas kernels for 0%

profile of v1, /device:TPU:504, one launch (start us, length us, event | category | flops | bytes accessed | tf_op | source)
XLA Modules:
  0.0 1399.5 jit_solution(17000625714931034058)
XLA Ops:
  9.6 12.1 all-to-all-start
  25.5 39.3 %all-to-all-done = bf16[64,1,24,2,128]{4,2,3,1,0:T(8,128)(2,1)S(1)} async-done(((bf16[64,1,24,2,128]{4,2,3,1,0:T(8,128)(2,1)}), bf16[64,1,24,2,128]{4,2,3,1,0:T(8,128)(2,1)S(1)}, u32[]{:S(2)}, u32[]{:S(2)}) %all-to-all-start) | async-done | bytes 786464 | tf_op jit(solution)/shard_map/all_to_all | solution.py:145
  77.3 87.2 %all-gather.3 = bf16[64,1,256]{2,1,0:T(2,128)(2,1)S(1)} all-gather(bf16[1,1,256]{2,1,0:T(2,128)(2,1)S(1)} %convert_bitcast_fusion.2), channel_id=2, replica_groups=mesh['pool'=64,'head'=8] {'pool'}, dimensions={0}, use_global_device_ids=true | all-gather | bytes 33280 | tf_op jit(solution)/shard_map/all_gather | solution.py:17
  164.5 78.4 %all-gather.4 = bf16[64,1,256]{2,1,0:T(2,128)(2,1)S(1)} all-gather(bf16[1,1,256]{2,1,0:T(2,128)(2,1)S(1)} %convert_bitcast_fusion.1), channel_id=3, replica_groups=mesh['pool'=64,'head'=8] {'pool'}, dimensions={0}, use_global_device_ids=true | all-gather | bytes 33280 | tf_op jit(solution)/shard_map/all_gather | solution.py:17
  244.4 1055.3 %while.35 = (s32[]{:T(128)}, f32[1,192]{1,0:T(1,128)S(1)}, f32[1,192]{1,0:T(1,128)S(1)}, f32[1,192,128]{2,1,0:T(8,128)S(1)}, s32[128]{0:T(128)S(1)}, /*index=5*/...) while((s32[]{:T(128)}, f32[1,192]{1,0:T(1,128)S(1)}, ...), condition=%wide.region_11.12_spmd.clone, body=%wide.region_6.11_spmd.clone.sunk | while | flops 6599373 | bytes 545140 | solution.py:195
  254.5 6.3 conditional.7
  281.1 6.3 conditional.7
  380.1 6.3 conditional.7
  401.6 6.3 conditional.7
  462.5 6.3 conditional.7
  546.2 6.3 conditional.7
  567.8 6.3 conditional.7
  584.3 6.3 conditional.7
  622.3 6.3 conditional.7
  666.7 6.3 conditional.7
  726.3 6.3 conditional.7
  742.8 6.3 conditional.7
  759.3 6.3 conditional.7
  786.0 6.3 conditional.7
  841.7 6.3 conditional.7
  858.2 6.3 conditional.7
  879.8 6.3 conditional.7
  906.4 6.3 conditional.7
  985.1 6.3 conditional.7
  1075.1 6.3 conditional.7
  1096.7 6.3 conditional.7
  1162.6 6.3 conditional.7
  1194.3 6.3 conditional.7
  1210.8 6.3 conditional.7
  1242.5 6.3 conditional.7
  1301.2 66.8 %while.34 = (s32[]{:T(128)}, f32[1,256]{1,0:T(1,128)S(1)}, f32[1,256]{1,0:T(1,128)S(1)}, f32[1,256,128]{2,1,0:T(8,128)S(1)}, bf16[64,1,256]{2,1,0:T(2,128)(2,1)S...) while((s32[]{:T(128)}, f32[1,256]{1,0:T(1,128)S(1)}, ...), condition=%wide.region_23.24_spmd, body=%wide.region_22.23_spmd.sunk | while | flops 133125 | bytes 337047 | solution.py:25
  1368.6 24.1 %psum.7 = bf16[32,128]{1,0:T(8,128)(2,1)} all-reduce(f32[32,128]{1,0:T(8,128)S(1)} %fusion.141), channel_id=1, replica_groups=mesh['pool'=64,'head'=8] {'head'}, use_global_device_ids=true, to_apply=%region_26.27 | all-reduce | flops 4096 | bytes 24576 | tf_op jit(solution)/shard_map/psum | solution.py:238
  (1740 shorter events, 817.8 us)
Async XLA Ops:
  7.2 1361.2 %copy-start = (bf16[1024,128]{1,0:T(8,128)(2,1)S(1)}, bf16[1024,128]{1,0:T(8,128)(2,1)}, u32[]{:S(2)}) copy-start(bf16[1024,128]{1,0:T(8,128)(2,1)} %param.26) | copy-start | bytes 786436
  7.2 237.2 %all-gather.8.cloned.1.call-start = ((), (), s32[]{:S(2)}) async-start(), calls=%async_computation.1 | async-start | bytes 4259840 | tf_op jit(solution)/shard_map/all_gather | solution.py:179
  8.6 13.2 copy-start.1
  8.6 13.3 copy-start.3
  8.6 13.4 copy-start.7
  9.6 12.6 copy-start.9
  9.6 14.5 %copy-start.6 = (s32[32]{0:T(128)S(1)}, s32[32]{0:T(128)}, u32[]{:S(2)}) copy-start(s32[32]{0:T(128)} %param.31) | copy-start | bytes 388
  9.6 14.7 %copy-start.8 = (s32[64]{0:T(128)S(1)}, s32[64]{0:T(128)}, u32[]{:S(2)}) copy-start(s32[64]{0:T(128)} %param.28) | copy-start | bytes 772
  9.6 15.9 %copy-start.2 = (bf16[2,2,64,128]{3,2,1,0:T(8,128)(2,1)S(1)}, bf16[2,2,64,128]{3,2,1,0:T(8,128)(2,1)}, u32[]{:S(2)}) copy-start(bf16[2,2,64,128]{3,2,1,0:T(8,128)(2,1)} %param.21) | copy-start | bytes 196612
  9.6 55.2 %all-to-all-start = ((bf16[64,1,24,2,128]{4,2,3,1,0:T(8,128)(2,1)}), bf16[64,1,24,2,128]{4,2,3,1,0:T(8,128)(2,1)S(1)}, u32[]{:S(2)}, u32[]{:S(2)}) async-start(bf16[64,1,24,2,128]{4,2,3,1,0:T(8,128)(2,1)} %stack.2), calls=%async_computation | async-start | bytes 1572864 | tf_op jit(solution)/shard_map/all_to_all | solution.py:145
  21.8 1278.6 %all-gather.10.cloned.1.call-start = ((), (), s32[]{:S(2)}) async-start(), calls=%async_computation.2 | async-start | bytes 4259840 | tf_op jit(solution)/shard_map/all_gather | solution.py:17
  68.9 6.1 copy-start.5
  69.2 7.9 copy-start.4
Sparse Core Ops, SparseCore 0:
  10.9 146.2 all-gather.7
  160.1 140.9 all-gather.9
